TPU v7x, 256 devices: a whole 4x4x8 slice. The times are simulated.
256 devices in a mesh: op: 8 (over z_lo, core), sec: 32 (over y, x, z_hi).
Axes of the slice: x: 4, y: 4, z: 8 (z_hi: 2, z_lo: 4; z = z_hi * 4 + z_lo), core: 2. Of those that a mesh axis runs over, the one named last changes fastest.
Arguments:
- psi: bfloat16 [3, 256, 256, 256], P(None, 'sec'), may hold values from -6 to 6
- left_ops: bfloat16 [32, 256, 256, 256], P('op', 'sec'), may hold values from -0.0625 to 0.0625
- right_ops: bfloat16 [32, 256, 256, 256], P('op', 'sec'), may hold values from -0.375 to 0.375
- shifts: int32 [32], P('op'), may hold values from -1 to 1
- active: int32 [32, 256], P('op', 'sec'), may hold values 0 or 1
Outputs:
- right_view: bfloat16 [3, 256, 256, 256], P(None, 'sec', None, 'op')
All inputs are finite; a program needn't handle non-finite values. No bound on the sum of `active` on one device may be relied on, other than what follows from the above.
Results may differ from a plain program's by a relative error of at most 0.0049.
Values may be sent and summed in bfloat16 or wider, within the bound.
A program may use at most 64 MiB of HBM per device.

v0:
```python
import jax
import jax.numpy as jnp
from jax import lax
from jax.sharding import PartitionSpec as P

QMAX = 1


def extended(value, sides, width):
    for axis, dim in sides:
        size, length = (lax.axis_size(axis), value.shape[dim])
        up = [(i, (i + 1) % size) for i in range(size - 1)]
        down = [(j, i) for i, j in up]
        last = lax.slice_in_dim(value, length - width, length, axis=dim)
        leading = lax.slice_in_dim(value, 0, width, axis=dim)
        before = lax.ppermute(last, axis, up)
        after = lax.ppermute(leading, axis, down)
        value = jnp.concatenate([before, value, after], axis=dim)
    return value


def per_device(psi, left_ops, right_ops, shifts, active):
    padded = extended(psi, (("sec", 1),), QMAX)
    count = left_ops.shape[0]
    sectors = psi.shape[1]
    nvec = psi.shape[0]
    blk = psi.shape[2]

    def add_term(index, total):
        start = QMAX - shifts[index]
        source = lax.dynamic_slice_in_dim(padded, start, sectors, 1)
        middle = jnp.einsum(
            "tij,vtjk->vtik", left_ops[index], source, preferred_element_type=jnp.float32
        ).astype(jnp.bfloat16)
        term = jnp.einsum(
            "vtik,tlk->vlti", middle, right_ops[index], preferred_element_type=jnp.float32
        )
        weight = active[index].astype(jnp.float32)
        return total + term * weight[None, None, :, None]

    total = lax.fori_loop(0, count, add_term, jnp.zeros((nvec, blk, sectors, blk), jnp.float32))
    summed = lax.psum(total, "op")
    share = blk // lax.axis_size("op")
    owned = lax.dynamic_slice_in_dim(summed, lax.axis_index("op") * share, share, 3)
    return lax.all_to_all(
        owned.astype(jnp.bfloat16), "sec", split_axis=1, concat_axis=2, tiled=True
    )


def solution(mesh):
    placed = (
        P(None, "sec", None, None),
        P("op", "sec", None, None),
        P("op", "sec", None, None),
        P("op"),
        P("op", "sec"),
    )
    return jax.shard_map(
        per_device,
        mesh=mesh,
        in_specs=placed,
        out_specs=P(None, "sec", None, "op"),
        check_vma=False,
    )
```

profile of v0, /device:TPU:1, one launch (start us, length us, event | category | flops | bytes accessed | tf_op | source)
XLA Modules:
  0.0 268.5 jit_solution(1910352454193892259)
XLA Ops:
  0.0 3.2 %copy.17 = bf16[3,8,256,256]{2,3,0,1:T(8,128)(2,1)S(1)} copy(bf16[3,8,256,256]{3,2,1,0:T(8,128)(2,1)} %param.7) | data formatting | bytes 6291456 | tf_op args[0]
  3.2 0.8 fusion.23
  4.0 10.4 %collective-permute-start = (bf16[3,1,256,256]{2,3,0,1:T(8,128)(2,1)}, bf16[3,1,256,256]{2,3,0,1:T(8,128)(2,1)}, u32[]{:S(2)}, u32[]{:S(2)}) collective-permute-start(bf16[3,1,256,256]{2,3,0,1:T(8,128)(2,1)} %get-tuple-element.220), channel_id=1, source_target_pairs={{0,1},{1,2},{2,3},{3,4},{4,5},{5,6},{6,7},{7,8},{8,9},{9,10},{10,1... | collective-permute-start | bytes 1179656 | tf_op jit(solution)/shard_map/ppermute | solution.py:16
  14.4 1.3 collective-permute-start.1
  15.7 7.2 %collective-permute-done = bf16[3,1,256,256]{2,3,0,1:T(8,128)(2,1)} collective-permute-done((bf16[3,1,256,256]{2,3,0,1:T(8,128)(2,1)}, bf16[3,1,256,256]{2,3,0,1:T(8,128)(2,1)}, u32[]{:S(2)}, u32[]{:S(2)}) %collective-permute-start) | collective-permute-done | bytes 393248 | tf_op jit(solution)/shard_map/ppermute | solution.py:16
  22.9 16.8 %collective-permute-done.1 = bf16[3,1,256,256]{2,3,0,1:T(8,128)(2,1)} collective-permute-done((bf16[3,1,256,256]{2,3,0,1:T(8,128)(2,1)S(1)}, bf16[3,1,256,256]{2,3,0,1:T(8,128)(2,1)}, u32[]{:S(2)}, u32[]{:S(2)}) %collective-permute-start.1) | collective-permute-done | bytes 393248 | tf_op jit(solution)/shard_map/ppermute | solution.py:17
  39.7 3.2 %pad_maximum_fusion = bf16[3,10,256,256]{2,3,0,1:T(8,128)(2,1)} fusion(bf16[3,1,256,256]{2,3,0,1:T(8,128)(2,1)} %collective-permute-done.1, bf16[3,8,256,256]{2,3,0,1:T(8,128)(2,1)S(1)} %copy.17, bf16[3,1,256,256]{2,3,0,1:T(8,128)(2,1)} %collective-permute-done), kind=kLoop, calls=%fused_computation.14 | loop fusion | flops 3932160 | bytes 7864320 | tf_op jit(solution)/shard_map/concatenate | solution.py:18
  42.9 44.0 %while.16 = (s32[]{:T(128)}, f32[3,256,8,256]{3,1,0,2:T(8,128)}, bf16[4,8,256,256]{3,2,1,0:T(8,128)(2,1)}, s32[4]{0:T(128)S(1)}, bf16[3,10,256,256]{2,3,0,1:T(8,...) while((s32[]{:T(128)}, f32[3,256,8,256]{3,1,0,2:T(8,128)}, ...), condition=%wide.region_1.0_spmd.clone, body=%wide.region_0.0_spmd.clone.sunk | while | flops 1616904192 | bytes 17827096 | solution.py:41
  42.9 0.6 dynamic_slice.93
  44.8 0.7 fusion.34
  45.5 7.0 %bitcast_add_fusion.2 = f32[3,256,8,256]{3,1,0,2:T(8,128)} fusion(f32[3,256,8,256]{3,1,0,2:T(8,128)} %get-tuple-element.277, f32[8]{0:T(128)S(1)} %fusion.34, pred[]{:T(512)S(6)} %compare.3, bf16[3,10,256,256]{2,3,0,1:T(8,128)(2,1)} %get-tuple-element.291, s32[]{:T(128)S(6)} %select_n.27, bf16[4,8,256,256]{3,2,1,0:T(8,128)(2,1)} %get-tuple-element.292, ...), kind=kOutput, calls=%fused_computation.clone.1 | convolution fusion | flops 1616904192 | bytes 17826852 | tf_op jit(solution)/shard_map/while/body/eval_jaxpr/vtik,tlk->vlti/dot_general | solution.py:35
  54.4 0.7 fusion.34
  55.1 8.9 %bitcast_add_fusion.2 = f32[3,256,8,256]{3,1,0,2:T(8,128)} fusion(f32[3,256,8,256]{3,1,0,2:T(8,128)} %get-tuple-element.277, f32[8]{0:T(128)S(1)} %fusion.34, pred[]{:T(512)S(6)} %compare.3, bf16[3,10,256,256]{2,3,0,1:T(8,128)(2,1)} %get-tuple-element.291, s32[]{:T(128)S(6)} %select_n.27, bf16[4,8,256,256]{3,2,1,0:T(8,128)(2,1)} %get-tuple-element.292, ...), kind=kOutput, calls=%fused_computation.clone.1 | convolution fusion | flops 1616904192 | bytes 17826852 | tf_op jit(solution)/shard_map/while/body/eval_jaxpr/vtik,tlk->vlti/dot_general | solution.py:35
  65.9 0.7 fusion.34
  66.6 8.9 %bitcast_add_fusion.2 = f32[3,256,8,256]{3,1,0,2:T(8,128)} fusion(f32[3,256,8,256]{3,1,0,2:T(8,128)} %get-tuple-element.277, f32[8]{0:T(128)S(1)} %fusion.34, pred[]{:T(512)S(6)} %compare.3, bf16[3,10,256,256]{2,3,0,1:T(8,128)(2,1)} %get-tuple-element.291, s32[]{:T(128)S(6)} %select_n.27, bf16[4,8,256,256]{3,2,1,0:T(8,128)(2,1)} %get-tuple-element.292, ...), kind=kOutput, calls=%fused_computation.clone.1 | convolution fusion | flops 1616904192 | bytes 17826852 | tf_op jit(solution)/shard_map/while/body/eval_jaxpr/vtik,tlk->vlti/dot_general | solution.py:35
  77.3 0.7 fusion.34
  78.0 8.9 %bitcast_add_fusion.2 = f32[3,256,8,256]{3,1,0,2:T(8,128)} fusion(f32[3,256,8,256]{3,1,0,2:T(8,128)} %get-tuple-element.277, f32[8]{0:T(128)S(1)} %fusion.34, pred[]{:T(512)S(6)} %compare.3, bf16[3,10,256,256]{2,3,0,1:T(8,128)(2,1)} %get-tuple-element.291, s32[]{:T(128)S(6)} %select_n.27, bf16[4,8,256,256]{3,2,1,0:T(8,128)(2,1)} %get-tuple-element.292, ...), kind=kOutput, calls=%fused_computation.clone.1 | convolution fusion | flops 1616904192 | bytes 17826852 | tf_op jit(solution)/shard_map/while/body/eval_jaxpr/vtik,tlk->vlti/dot_general | solution.py:35
  86.9 9.1 %copy.20 = f32[3,256,8,256]{3,2,0,1:T(8,128)} copy(f32[3,256,8,256]{3,1,0,2:T(8,128)} %get-tuple-element.181) | data formatting | bytes 12582912 | tf_op jit(solution)/shard_map/while | solution.py:41
  96.0 132.5 %all-reduce.1 = bf16[3,256,8,256]{3,2,0,1:T(8,128)(2,1)S(1)} all-reduce(f32[3,256,8,256]{3,2,0,1:T(8,128)} %copy.20), channel_id=1, replica_groups=mesh['op'=8,'sec'=32] {'op'}, use_global_device_ids=true, to_apply=%region_2.0 | all-reduce | flops 1572864 | bytes 9437184 | tf_op jit(solution)/shard_map/psum | solution.py:42
  228.5 1.7 fusion.24
  230.2 3.1 %reshape.17 = bf16[32,2,3072]{2,1,0:T(2,128)(2,1)S(1)} reshape(bf16[256,3,8,32]{3,2,1,0:T(8,128)(2,1)} %fusion.24) | data formatting | bytes 786432
  233.2 32.8 %all_to_all.18 = bf16[32,2,3072]{2,1,0:T(2,128)(2,1)S(1)} all-to-all(bf16[32,2,3072]{2,1,0:T(2,128)(2,1)S(1)} %reshape.17), channel_id=1, replica_groups=mesh['op'=8,'sec'=32] {'sec'}, dimensions={0} | all-to-all | bytes 786432 | tf_op jit(solution)/shard_map/all_to_all | solution.py:45
  266.0 0.7 reshape.18
  267.2 1.3 copy.22
  (7 shorter events, 2.2 us)
Async XLA Ops:
  4.0 18.9 %collective-permute-start = (bf16[3,1,256,256]{2,3,0,1:T(8,128)(2,1)}, bf16[3,1,256,256]{2,3,0,1:T(8,128)(2,1)}, u32[]{:S(2)}, u32[]{:S(2)}) collective-permute-start(bf16[3,1,256,256]{2,3,0,1:T(8,128)(2,1)} %get-tuple-element.220), channel_id=1, source_target_pairs={{0,1},{1,2},{2,3},{3,4},{4,5},{5,6},{6,7},{7,8},{8,9},{9,10},{10,1... | collective-permute-start | bytes 1179656 | tf_op jit(solution)/shard_map/ppermute | solution.py:16
  14.4 25.3 %collective-permute-start.1 = (bf16[3,1,256,256]{2,3,0,1:T(8,128)(2,1)S(1)}, bf16[3,1,256,256]{2,3,0,1:T(8,128)(2,1)}, u32[]{:S(2)}, u32[]{:S(2)}) collective-permute-start(bf16[3,1,256,256]{2,3,0,1:T(8,128)(2,1)S(1)} %get-tuple-element.221), channel_id=1, source_target_pairs={{1,0},{2,1},{3,2},{4,3},{5,4},{6,5},{7,6},{8,7},{9,8},{10,9},{11,1... | collective-permute-start | bytes 1179656 | tf_op jit(solution)/shard_map/ppermute | solution.py:17
  15.7 27.2 %copy-start = (s32[4]{0:T(128)S(1)}, s32[4]{0:T(128)}, u32[]{:S(2)}) copy-start(s32[4]{0:T(128)} %param.10) | copy-start | bytes 52
where the time goes:
time: 269 us
  blocking collectives  165 us (61%)
  matrix products  33.7 us (13%)
  waiting for transfers between devices  24 us (9%)
  local copies, waits for them, and re-layouts  22.6 us (8%)
  starting transfers between devices  11.7 us (4%)
  other arithmetic  6 us (2%)
  loops' own time  5.21 us (2%)
    psum x1, blocking collectives, per_device(): summed = lax.psum(total, 'op')  132 us
    dot_general x4, matrix products, add_term(): jnp.einsum('vtik,tlk->vlti', middle, right_ops[index], preferred_element_...  33.7 us
    all_to_all x1, blocking collectives, per_device(): lax.all_to_all(owned.astype(jnp.bfloat16), 'sec', split_axis=1, concat_ax...  32.8 us
    ppermute x1, waiting for transfers between devices, extended(): after = lax.ppermute(leading, axis, down)  16.8 us
    ppermute x1, starting transfers between devices, extended(): before = lax.ppermute(last, axis, up)  10.4 us
    while x1, local copies, waits for them, and re-layouts, per_device(): lax.fori_loop(0, count, add_term, jnp.zeros((nvec, blk, sectors, blk), jn...  9.08 us
    unnamed x6, local copies, waits for them, and re-layouts  8.67 us
    ppermute x1, waiting for transfers between devices, extended(): before = lax.ppermute(last, axis, up)  7.21 us
  transfers between devices with their start and end apart: 2, of which 2 were waited for; matrix products, arithmetic and copies ran while one was open for 0% of the time, Pallas kernels for 0%

commit v1 on v0

--- a/solution.py
+++ b/solution.py
@@ -4,6 +4,13 @@
 from jax.sharding import PartitionSpec as P
 
 QMAX = 1
+
+
+def stacked_exchange(shard, axis, split, join):
+    count = lax.axis_size(axis)
+    blocks = jnp.stack(jnp.split(shard, count, axis=split), axis=0)
+    blocks = lax.all_to_all(blocks, axis, split_axis=0, concat_axis=0)
+    return jnp.concatenate(blocks, axis=join)
 
 
 def extended(value, sides, width):
@@ -42,9 +49,7 @@
     summed = lax.psum(total, "op")
     share = blk // lax.axis_size("op")
     owned = lax.dynamic_slice_in_dim(summed, lax.axis_index("op") * share, share, 3)
-    return lax.all_to_all(
-        owned.astype(jnp.bfloat16), "sec", split_axis=1, concat_axis=2, tiled=True
-    )
+    return stacked_exchange(owned.astype(jnp.bfloat16), "sec", 1, 2)
 
 
 def solution(mesh):

time: 269 us -> 254 us (0.944)
  local copies, waits for them, and re-layouts: 22.6 us -> 8.52 us
    while x1 -> x0, local copies, waits for them, and re-layouts: 9.08 us -> none  [per_device(): lax.fori_loop(0, count, add_term, jnp.zeros((nvec, blk, sectors, blk), jn...]
    unnamed x6 -> x35, local copies, waits for them, and re-layouts: 8.67 us -> 2.96 us
where the time goes in v1:
time: 254 us
  blocking collectives  165 us (65%)
  matrix products  33.5 us (13%)
  waiting for transfers between devices  24.4 us (10%)
  starting transfers between devices  11 us (4%)
  local copies, waits for them, and re-layouts  8.52 us (3%)
  other arithmetic  6.39 us (3%)
  loops' own time  4.51 us (2%)
    psum x1, blocking collectives, per_device(): summed = lax.psum(total, 'op')  132 us
    dot_general x4, matrix products, add_term(): jnp.einsum('vtik,tlk->vlti', middle, right_ops[index], preferred_element_...  33.5 us
    all_to_all x1, blocking collectives, stacked_exchange(): blocks = lax.all_to_all(blocks, axis, split_axis=0, concat_axis=0)  32.8 us
    ppermute x1, waiting for transfers between devices, extended(): after = lax.ppermute(leading, axis, down)  16.8 us
    ppermute x1, starting transfers between devices, extended(): before = lax.ppermute(last, axis, up)  9.67 us
    ppermute x1, waiting for transfers between devices, extended(): before = lax.ppermute(last, axis, up)  7.64 us
  transfers between devices with their start and end apart: 2, of which 2 were waited for; matrix products, arithmetic and copies ran while one was open for 0% of the time, Pallas kernels for 0%

profile of v1, /device:TPU:1, one launch (start us, length us, event | category | flops | bytes accessed | tf_op | source)
XLA Modules:
  0.0 253.8 jit_solution(15677542073709868371)
XLA Ops:
  0.0 1.2 fusion.23
  1.2 9.7 %collective-permute-start = (bf16[3,1,256,256]{3,2,1,0:T(8,128)(2,1)S(1)}, bf16[3,1,256,256]{3,2,1,0:T(8,128)(2,1)S(1)}, u32[]{:S(2)}, u32[]{:S(2)}) collective-permute-start(bf16[3,1,256,256]{3,2,1,0:T(8,128)(2,1)S(1)} %get-tuple-element.220), channel_id=1, source_target_pairs={{0,1},{1,2},{2,3},{3,4},{4,5},{5,6},{6,7},{7,8},{8,9},{9,10},{10,1... | collective-permute-start | bytes 1179656 | tf_op jit(solution)/shard_map/ppermute | solution.py:23
  10.8 1.3 collective-permute-start.1
  12.2 7.6 %collective-permute-done = bf16[3,1,256,256]{3,2,1,0:T(8,128)(2,1)S(1)} collective-permute-done((bf16[3,1,256,256]{3,2,1,0:T(8,128)(2,1)S(1)}, bf16[3,1,256,256]{3,2,1,0:T(8,128)(2,1)S(1)}, u32[]{:S(2)}, u32[]{:S(2)}) %collective-permute-start) | collective-permute-done | bytes 393248 | tf_op jit(solution)/shard_map/ppermute | solution.py:23
  19.8 16.8 %collective-permute-done.1 = bf16[3,1,256,256]{3,2,1,0:T(8,128)(2,1)S(1)} collective-permute-done((bf16[3,1,256,256]{3,2,1,0:T(8,128)(2,1)S(1)}, bf16[3,1,256,256]{3,2,1,0:T(8,128)(2,1)S(1)}, u32[]{:S(2)}, u32[]{:S(2)}) %collective-permute-start.1) | collective-permute-done | bytes 393248 | tf_op jit(solution)/shard_map/ppermute | solution.py:24
  36.6 3.6 %pad_maximum_fusion = bf16[3,10,256,256]{3,2,1,0:T(8,128)(2,1)} fusion(bf16[3,1,256,256]{3,2,1,0:T(8,128)(2,1)S(1)} %collective-permute-done.1, bf16[3,8,256,256]{3,2,1,0:T(8,128)(2,1)} %param.7, bf16[3,1,256,256]{3,2,1,0:T(8,128)(2,1)S(1)} %collective-permute-done), kind=kLoop, calls=%fused_computation.15 | loop fusion | flops 3932160 | bytes 7864320 | tf_op jit(solution)/shard_map/concatenate | solution.py:25
  40.2 43.1 %while.16 = (s32[]{:T(128)}, f32[3,256,8,256]{3,1,0,2:T(8,128)}, bf16[4,8,256,256]{3,2,1,0:T(8,128)(2,1)}, s32[4]{0:T(128)S(1)}, bf16[3,10,256,256]{3,2,1,0:T(8,...) while((s32[]{:T(128)}, f32[3,256,8,256]{3,1,0,2:T(8,128)}, ...), condition=%wide.region_1.0_spmd.clone, body=%wide.region_0.0_spmd.clone.sunk | while | flops 1616904192 | bytes 17827096 | solution.py:48
  40.2 0.6 dynamic_slice.87
  41.9 0.7 fusion.33
  42.6 7.0 %bitcast_add_fusion.2 = f32[3,256,8,256]{3,1,0,2:T(8,128)} fusion(f32[3,256,8,256]{3,1,0,2:T(8,128)} %get-tuple-element.277, f32[8]{0:T(128)S(1)} %fusion.33, pred[]{:T(512)S(6)} %compare.3, bf16[4,8,256,256]{3,2,1,0:T(8,128)(2,1)} %get-tuple-element.292, s32[]{:T(128)} %get-tuple-element.276, bf16[4,8,256,256]{3,2,1,0:T(8,128)(2,1)} %get-tuple-element.289, ...), kind=kOutput, calls=%fused_computation.clone.1 | convolution fusion | flops 1616904192 | bytes 17826852 | tf_op jit(solution)/shard_map/while/body/eval_jaxpr/vtik,tlk->vlti/dot_general | solution.py:42
  49.6 0.6 dynamic_slice.87
  51.3 0.7 fusion.33
  52.0 8.8 %bitcast_add_fusion.2 = f32[3,256,8,256]{3,1,0,2:T(8,128)} fusion(f32[3,256,8,256]{3,1,0,2:T(8,128)} %get-tuple-element.277, f32[8]{0:T(128)S(1)} %fusion.33, pred[]{:T(512)S(6)} %compare.3, bf16[4,8,256,256]{3,2,1,0:T(8,128)(2,1)} %get-tuple-element.292, s32[]{:T(128)} %get-tuple-element.276, bf16[4,8,256,256]{3,2,1,0:T(8,128)(2,1)} %get-tuple-element.289, ...), kind=kOutput, calls=%fused_computation.clone.1 | convolution fusion | flops 1616904192 | bytes 17826852 | tf_op jit(solution)/shard_map/while/body/eval_jaxpr/vtik,tlk->vlti/dot_general | solution.py:42
  60.8 0.6 dynamic_slice.87
  62.5 0.7 fusion.33
  63.2 8.8 %bitcast_add_fusion.2 = f32[3,256,8,256]{3,1,0,2:T(8,128)} fusion(f32[3,256,8,256]{3,1,0,2:T(8,128)} %get-tuple-element.277, f32[8]{0:T(128)S(1)} %fusion.33, pred[]{:T(512)S(6)} %compare.3, bf16[4,8,256,256]{3,2,1,0:T(8,128)(2,1)} %get-tuple-element.292, s32[]{:T(128)} %get-tuple-element.276, bf16[4,8,256,256]{3,2,1,0:T(8,128)(2,1)} %get-tuple-element.289, ...), kind=kOutput, calls=%fused_computation.clone.1 | convolution fusion | flops 1616904192 | bytes 17826852 | tf_op jit(solution)/shard_map/while/body/eval_jaxpr/vtik,tlk->vlti/dot_general | solution.py:42
  72.1 0.6 dynamic_slice.87
  73.8 0.7 fusion.33
  74.4 8.8 %bitcast_add_fusion.2 = f32[3,256,8,256]{3,1,0,2:T(8,128)} fusion(f32[3,256,8,256]{3,1,0,2:T(8,128)} %get-tuple-element.277, f32[8]{0:T(128)S(1)} %fusion.33, pred[]{:T(512)S(6)} %compare.3, bf16[4,8,256,256]{3,2,1,0:T(8,128)(2,1)} %get-tuple-element.292, s32[]{:T(128)} %get-tuple-element.276, bf16[4,8,256,256]{3,2,1,0:T(8,128)(2,1)} %get-tuple-element.289, ...), kind=kOutput, calls=%fused_computation.clone.1 | convolution fusion | flops 1616904192 | bytes 17826852 | tf_op jit(solution)/shard_map/while/body/eval_jaxpr/vtik,tlk->vlti/dot_general | solution.py:42
  83.3 132.5 %all-reduce.1 = bf16[3,256,8,256]{3,1,0,2:T(8,128)(2,1)S(1)} all-reduce(f32[3,256,8,256]{3,1,0,2:T(8,128)} %get-tuple-element.181), channel_id=1, replica_groups=mesh['op'=8,'sec'=32] {'op'}, use_global_device_ids=true, to_apply=%region_2.0 | all-reduce | flops 1572864 | bytes 9437184 | tf_op jit(solution)/shard_map/psum | solution.py:49
  217.2 1.5 reshape.25
  218.7 32.8 %all_to_all.5 = bf16[32,2,3072]{2,1,0:T(2,128)(2,1)S(1)} all-to-all(bf16[32,2,3072]{2,1,0:T(2,128)(2,1)S(1)} %reshape.25), channel_id=1, replica_groups=mesh['op'=8,'sec'=32] {'sec'}, dimensions={0} | all-to-all | bytes 786432 | tf_op jit(solution)/shard_map/all_to_all | solution.py:12
  251.5 0.7 reshape.26
  252.2 1.6 copy.8
  (36 shorter events, 1.3 us)
Async XLA Ops:
  1.2 18.6 %collective-permute-start = (bf16[3,1,256,256]{3,2,1,0:T(8,128)(2,1)S(1)}, bf16[3,1,256,256]{3,2,1,0:T(8,128)(2,1)S(1)}, u32[]{:S(2)}, u32[]{:S(2)}) collective-permute-start(bf16[3,1,256,256]{3,2,1,0:T(8,128)(2,1)S(1)} %get-tuple-element.220), channel_id=1, source_target_pairs={{0,1},{1,2},{2,3},{3,4},{4,5},{5,6},{6,7},{7,8},{8,9},{9,10},{10,1... | collective-permute-start | bytes 1179656 | tf_op jit(solution)/shard_map/ppermute | solution.py:23
  10.8 25.7 %collective-permute-start.1 = (bf16[3,1,256,256]{3,2,1,0:T(8,128)(2,1)S(1)}, bf16[3,1,256,256]{3,2,1,0:T(8,128)(2,1)S(1)}, u32[]{:S(2)}, u32[]{:S(2)}) collective-permute-start(bf16[3,1,256,256]{3,2,1,0:T(8,128)(2,1)S(1)} %get-tuple-element.221), channel_id=1, source_target_pairs={{1,0},{2,1},{3,2},{4,3},{5,4},{6,5},{7,6},{8,7},{9,8},{10,9},{11,1... | collective-permute-start | bytes 1179656 | tf_op jit(solution)/shard_map/ppermute | solution.py:24
  12.2 28.0 %copy-start = (s32[4]{0:T(128)S(1)}, s32[4]{0:T(128)}, u32[]{:S(2)}) copy-start(s32[4]{0:T(128)} %param.10) | copy-start | bytes 52
